TPU v7x, 128 devices: a whole 4x4x4 slice. The times are simulated.
128 devices in a mesh: member: 32 (over x, z, core), mp: 4 (over y).
Axes of the slice: x: 4, y: 4, z: 4, core: 2. Of those that a mesh axis runs over, the one named last changes fastest.
Arguments:
- latents: bfloat16 [128, 1024, 1024], P('member', 'mp'), may hold values from -6 to 6
- w_first: bfloat16 [1024, 2048], P(None, 'mp'), may hold values from -0.1875 to 0.1875
- w_second: bfloat16 [2048, 1024], P('mp'), may hold values from -0.125 to 0.125
- readout_matrix: bfloat16 [1024, 768], P(None, 'mp'), may hold values from -0.1875 to 0.1875
- observed: float32 [1024, 768], P(('mp', 'member')), may hold values from -9 to 9
- obs_index: int32 [1024], P(('mp', 'member')), may hold values from 0 to 1023, as said below
- valid_mask: int32 [1024], P(('mp', 'member')), may hold values from 0 to 1
Outputs:
- grad_first: float32 [1024, 2048], P(('member', 'mp'))
- grad_second: float32 [2048, 1024], P(('member', 'mp'))
- grad_head: float32 [1024, 768], P(('member', 'mp'))
- loss: float32 [], replicated
Inputs may be any that keep to these rules, and one draw needn't show every extreme that they name: obs_index[p] names a record of the same aligned block of 8 patches as p.
All inputs are finite; a program needn't handle non-finite values.
Results may differ from a plain program's by a relative error of at most 0.006.
Values may be sent and summed in bfloat16 or wider, within the bound.
No kernel may reach another device: no remote copies, remote signals or barrier semaphores. Data moves between devices by JAX's collectives and lax.ppermute only.
A program may use at most 128 MiB of HBM per device.

v0:
```python
import jax
import jax.numpy as jnp
from jax import lax
from jax.sharding import PartitionSpec as P

SMOOTHING = 1.0
LOSS_SCALE = 4096.0


def split_up(x, dim, devices):
    lengths = x.shape
    parts = x.reshape(*lengths[:dim], devices, lengths[dim] // devices, *lengths[dim + 1 :])
    return jnp.moveaxis(parts, dim, 0)


def sent_and_summed(x, axis, dim):
    parts = split_up(x, dim, lax.axis_size(axis))
    arrived = lax.all_to_all(parts, axis, split_axis=0, concat_axis=0, tiled=True)
    return arrived.sum(axis=0)


def in_order(parts, dim):
    parts = jnp.moveaxis(parts, 0, dim)
    lengths = parts.shape
    return parts.reshape(*lengths[:dim], lengths[dim] * lengths[dim + 1], *lengths[dim + 2 :])


def one_gather(arrays, axis, dims):
    vector = jnp.concatenate([a.reshape(-1) for a in arrays])
    lines, at, outs = (lax.all_gather(vector, axis), 0, [])
    for a, dim in zip(arrays, dims):
        parts = lines[:, at : at + a.size].reshape(-1, *a.shape)
        outs.append(in_order(parts, dim))
        at += a.size
    return tuple(outs)


def gelu_fn(values):
    return jax.nn.gelu(values, approximate=True)


def gelu_back(preact, upstream):
    return jax.vjp(gelu_fn, preact)[1](upstream)[0]


def row_outer(left_rows, right_rows):
    return lax.dot_general(
        left_rows, right_rows, (((0,), (0,)), ((), ())), preferred_element_type=jnp.float32
    )


def weight_sum(left_rows, right_rows):
    across = lax.axis_size("member")
    within = lax.axis_size("mp")
    share_rows = left_rows.shape[1] // (across * within)
    local_grad = row_outer(left_rows, right_rows)
    reordered = (
        local_grad.reshape(across, within, share_rows, -1)
        .transpose(1, 0, 2, 3)
        .reshape(left_rows.shape[1], -1)
    )
    group_sum = lax.psum_scatter(reordered, "mp", scatter_dimension=0, tiled=True)
    return sent_and_summed(group_sum, "member", 0)


def per_device(latents, w_first, w_second, readout_matrix, observed, obs_index, valid_mask):
    sample_portion, tile_portion, feature_width = latents.shape
    full_first, full_second, complete_head = one_gather(
        (w_first, w_second, readout_matrix), "mp", (1, 0, 1)
    )
    token_rows = latents.reshape(sample_portion * tile_portion, feature_width)
    preact = jnp.dot(token_rows, full_first, preferred_element_type=jnp.float32)
    hidden = gelu_fn(preact).astype(jnp.bfloat16)
    skip_activation = (
        token_rows.astype(jnp.float32)
        + jnp.dot(hidden, full_second, preferred_element_type=jnp.float32)
    ).astype(jnp.bfloat16)
    prediction_lines = jnp.dot(
        skip_activation, complete_head, preferred_element_type=jnp.float32
    ).astype(jnp.bfloat16)
    prediction_lines = prediction_lines.reshape(sample_portion, tile_portion, -1)
    ensemble_reduced = lax.all_to_all(
        prediction_lines, "member", split_axis=1, concat_axis=0, tiled=True
    )
    sample_indices = ensemble_reduced.shape[0]
    owned_count = ensemble_reduced.shape[1]
    offset_row = (
        lax.axis_index("mp") * lax.axis_size("member") + lax.axis_index("member")
    ) * owned_count
    target = jnp.take(observed, obs_index - offset_row, axis=0)
    predicted_samples = ensemble_reduced.astype(jnp.float32)
    gram_matrix = jnp.einsum(
        "mpo,npo->pmn", ensemble_reduced, ensemble_reduced, preferred_element_type=jnp.float32
    )
    squares = jnp.sum(predicted_samples * predicted_samples, axis=2).T
    dist_sq = squares[:, :, None] + squares[:, None, :] - 2.0 * gram_matrix
    spread = jnp.sqrt(dist_sq + SMOOTHING)
    kernel = 1.0 / spread
    kernel_sum = jnp.sum(kernel, axis=2)
    pulled = jnp.einsum("pmn,npo->mpo", kernel, predicted_samples, precision=lax.Precision.HIGHEST)
    offset = predicted_samples - target[None]
    error_norm = jnp.sqrt(jnp.sum(offset * offset, axis=2) + SMOOTHING)
    repulse = predicted_samples * kernel_sum.T[:, :, None] - pulled
    validity = valid_mask.astype(jnp.float32)
    grad_raw = (
        LOSS_SCALE
        * validity[None, :, None]
        * (
            offset / (sample_indices * error_norm[:, :, None])
            - repulse / (sample_indices * sample_indices)
        )
    ).astype(jnp.bfloat16)
    scores = validity * (
        jnp.mean(error_norm, axis=0)
        - jnp.sum(spread, axis=(1, 2)) / (2.0 * sample_indices * sample_indices)
    )
    score_part = jnp.sum(scores)
    count_part = jnp.sum(validity)
    valid_count = lax.psum(count_part, ("member", "mp"))
    returned = lax.all_to_all(grad_raw, "member", split_axis=0, concat_axis=1, tiled=True)
    grad_rows = returned.reshape(sample_portion * tile_portion, -1)
    resid_grad = jnp.dot(grad_rows, complete_head.T, preferred_element_type=jnp.float32).astype(
        jnp.bfloat16
    )
    hidden_grad = jnp.dot(resid_grad, full_second.T, preferred_element_type=jnp.float32)
    preact_grad = gelu_back(preact, hidden_grad).astype(jnp.bfloat16)
    sum_first = weight_sum(token_rows, preact_grad)
    sum_second = weight_sum(hidden, resid_grad)
    sum_head = weight_sum(skip_activation, grad_rows)
    score_total = lax.psum(score_part, ("member", "mp"))
    valid_total = jnp.maximum(valid_count, 1.0)
    grad_scale = 1.0 / valid_total
    return (
        sum_first * grad_scale,
        sum_second * grad_scale,
        sum_head * grad_scale,
        score_total / valid_total,
    )


def solution(mesh):
    return jax.shard_map(
        per_device,
        mesh=mesh,
        in_specs=(
            P("member", "mp", None),
            P(None, "mp"),
            P("mp", None),
            P(None, "mp"),
            P(("mp", "member"), None),
            P(("mp", "member")),
            P(("mp", "member")),
        ),
        out_specs=(
            P(("member", "mp"), None),
            P(("member", "mp"), None),
            P(("member", "mp"), None),
            P(),
        ),
        check_vma=False,
    )
```

profile of v0, /device:TPU:1, one launch (start us, length us, event | category | flops | bytes accessed | tf_op | source)
XLA Modules:
  0.0 563.1 jit_solution(6890008387283289417)
XLA Ops:
  11.1 14.1 %pad_maximum_fusion = bf16[1245184]{0:T(1024)(128)(2,1)} fusion(bf16[196608]{0:T(1024)(128)(2,1)S(1)} %reshape.107, bf16[524288]{0:T(1024)(128)(2,1)S(1)} %bitcast.110, bf16[524288]{0:T(1024)(128)(2,1)S(1)} %bitcast.109), kind=kLoop, calls=%fused_computation.31 | loop fusion | flops 7471104 | bytes 4980736 | tf_op jit(solution)/shard_map/concatenate | solution.py:29
  27.8 97.2 %all-gather.3.cloned.1.call-done = bf16[4980736]{0:T(1024)(128)(2,1)} async-done(((bf16[1245184]{0:T(1024)(128)(2,1)}), bf16[4980736]{0:T(1024)(128)(2,1)}) %all-gather.3.cloned.1.call-update) | async-done | bytes 9961488 | tf_op jit(solution)/shard_map/all_gather | solution.py:30
  125.0 13.0 %reshape.130 = bf16[4,1245184]{1,0:T(4,128)(2,1)} reshape(bf16[4980736]{0:T(1024)(128)(2,1)} %all-gather.3.cloned.1.call-done) | data formatting | bytes 19922944 | tf_op jit(solution)/shard_map/all_gather | solution.py:30
  137.9 8.3 %fusion.38 = (bf16[4,524288]{1,0:T(4,128)(2,1)}, bf16[4,524288]{1,0:T(4,128)(2,1)}) fusion(bf16[4,1245184]{1,0:T(4,128)(2,1)} %reshape.130), kind=kLoop, calls=%fused_computation.64 | loop fusion | bytes 16777216 | tf_op jit(solution)/shard_map/slice | solution.py:32
  146.3 8.0 %reshape_reshape.3 = bf16[2048,1024]{1,0:T(8,128)(2,1)} reshape(bf16[4,524288]{1,0:T(4,128)(2,1)} %get-tuple-element.14) | data formatting | bytes 8388608 | tf_op jit(solution)/shard_map/reshape;reshape | solution.py:25
  154.3 5.0 copy.110
  159.3 6.4 %copy.75 = bf16[1024,4,512]{0,2,1:T(8,128)(2,1)} copy(bf16[1024,4,512]{2,0,1:T(8,128)(2,1)} %bitcast.101) | data formatting | bytes 8388608 | tf_op jit(solution)/shard_map/transpose | solution.py:23
  165.7 2.8 reshape.133
  168.4 3.1 reshape.110
  173.9 7.1 %fusion.41 = f32[2048,1024]{1,0:T(8,128)S(1)} fusion(bf16[1024,2048]{0,1:T(8,128)(2,1)} %bitcast.111, bf16[1024,1024]{1,0:T(8,128)(2,1)} %bitcast.112), kind=kOutput, calls=%fused_computation.66 | convolution fusion | flops 4294967296 | bytes 14680064 | tf_op jit(solution)/shard_map/dot_general | solution.py:72
  181.1 5.2 add_convert_fusion
  190.6 7.7 %all-to-all-start = ((bf16[4,256,768]{2,0,1:T(4,128)(2,1)}), bf16[4,256,768]{2,0,1:T(4,128)(2,1)S(1)}, u32[]{:S(2)}, u32[]{:S(2)}) async-start(bf16[4,256,768]{2,0,1:T(4,128)(2,1)} %copy.77), calls=%async_computation | async-start | bytes 3145728 | tf_op jit(solution)/shard_map/all_to_all | solution.py:82
  199.1 21.9 %all-to-all-done = bf16[4,256,768]{2,0,1:T(4,128)(2,1)S(1)} async-done(((bf16[4,256,768]{2,0,1:T(4,128)(2,1)}), bf16[4,256,768]{2,0,1:T(4,128)(2,1)S(1)}, u32[]{:S(2)}, u32[]{:S(2)}) %all-to-all-start) | async-done | bytes 1572896 | tf_op jit(solution)/shard_map/all_to_all | solution.py:82
  229.3 26.9 %all_to_all.48 = bf16[128,8,768]{2,1,0:T(8,128)(2,1)S(1)} all-to-all(bf16[128,8,768]{2,1,0:T(8,128)(2,1)S(1)} %copy.88), channel_id=1, replica_groups=mesh['member'=32,'mp'=4] {'member'}, dimensions={0} | all-to-all | bytes 3145728 | tf_op jit(solution)/shard_map/all_to_all | solution.py:120
  262.0 8.3 %fusion.34 = f32[2048,1024]{1,0:T(8,128)S(1)} fusion(bf16[1024,1024]{1,0:T(8,128)(2,1)S(1)} %convolution_convert_fusion, f32[2048,1024]{1,0:T(8,128)} %copy-done.14), kind=kOutput, calls=%fused_computation.62 | convolution fusion | flops 4313841664 | bytes 18874368 | tf_op jit(solution)/shard_map/dot_general | solution.py:47
  270.3 4.1 copy.93
  276.0 16.7 %fusion.10 = f32[2048,1024]{0,1:T(8,128)} fusion(bf16[1024,1024]{1,0:T(8,128)(2,1)S(1)} %bitcast.114, f32[2048,1024]{1,0:T(8,128)} %copy-done.14, bf16[1024,1024]{1,0:T(8,128)(2,1)} %copy-done.13, bf16[2048,1024]{1,0:T(8,128)(2,1)} %reshape_reshape.3), kind=kOutput, calls=%fused_computation.17 | convolution fusion | flops 8631877632 | bytes 25165824 | tf_op jit(solution)/shard_map/dot_general | solution.py:47
  292.7 7.8 %copy.92 = f32[32,4,8,2048]{3,2,0,1:T(8,128)} copy(f32[32,4,8,2048]{3,2,1,0:T(8,128)} %bitcast.106) | data formatting | bytes 16777216 | tf_op jit(solution)/shard_map/reshape | solution.py:58
  300.5 17.8 %all_to_all.49 = f32[32,8,768]{2,1,0:T(8,128)S(1)} all-to-all(f32[32,8,768]{2,1,0:T(8,128)} %bitcast.124), channel_id=1, replica_groups=mesh['member'=32,'mp'=4] {'member'}, dimensions={0} | all-to-all | bytes 1572864 | tf_op jit(solution)/shard_map/all_to_all | solution.py:18
  318.4 59.9 %reduce-scatter.6.cloned.1.call-done = f32[512,1024]{1,0:T(8,128)} async-done(((f32[2048,1024]{1,0:T(8,128)}), f32[512,1024]{1,0:T(8,128)}) %reduce-scatter.6.cloned.1.call-update) | async-done | bytes 2097168 | tf_op jit(solution)/shard_map/reduce_scatter | solution.py:62
  378.3 7.6 %all-to-all-start.3 = ((f32[32,16,1024]{2,1,0:T(8,128)}), f32[32,16,1024]{2,1,0:T(8,128)S(1)}, u32[]{:S(2)}, u32[]{:S(2)}) async-start(f32[32,16,1024]{2,1,0:T(8,128)} %bitcast.116), calls=%async_computation.5 | async-start | bytes 4194304 | tf_op jit(solution)/shard_map/all_to_all | solution.py:18
  385.9 75.0 %reduce-scatter.4.cloned.1.call-done = f32[256,2048]{1,0:T(8,128)} async-done(((f32[1024,2048]{1,0:T(8,128)}), f32[256,2048]{1,0:T(8,128)}) %reduce-scatter.4.cloned.1.call-update) | async-done | bytes 2097168 | tf_op jit(solution)/shard_map/reduce_scatter | solution.py:62
  460.9 7.8 %all-to-all-start.2 = ((f32[32,8,2048]{2,1,0:T(8,128)}), f32[32,8,2048]{2,1,0:T(8,128)}, u32[]{:S(2)}, u32[]{:S(2)}) async-start(f32[32,8,2048]{2,1,0:T(8,128)} %bitcast.115), calls=%async_computation.3 | async-start | bytes 4194304 | tf_op jit(solution)/shard_map/all_to_all | solution.py:18
  468.7 81.5 %all-reduce = (f32[]{:T(128)}, f32[]{:T(128)}) all-reduce(f32[]{:T(128)} %get-tuple-element.9, f32[]{:T(128)} %get-tuple-element.8), channel_id=1, replica_groups=mesh['member'=32,'mp'=4] {'member','mp'}, use_global_device_ids=true, to_apply=%region_6.7 | all-reduce | flops 2 | bytes 16 | tf_op jit(solution)/shard_map/psum | solution.py:119
  (78 shorter events, 33.2 us)
Async XLA Ops:
  7.2 191.2 %copy-start = (f32[8,768]{1,0:T(8,128)S(1)}, f32[8,768]{1,0:T(8,128)}, u32[]{:S(2)}) copy-start(f32[8,768]{1,0:T(8,128)} %param.11) | copy-start | bytes 73732
  7.2 3.6 copy-start.8
  7.2 117.8 %all-gather.3.cloned.1.call-start = ((), (), s32[]{:S(2)}) async-start(), calls=%async_computation.11 | async-start | bytes 12451840 | tf_op jit(solution)/shard_map/all_gather | solution.py:30
  11.1 14.1 %copy-start.3 = (bf16[4,256,1024]{2,1,0:T(8,128)(2,1)S(1)}, bf16[4,256,1024]{2,1,0:T(8,128)(2,1)}, u32[]{:S(2)}) copy-start(bf16[4,256,1024]{2,1,0:T(8,128)(2,1)} %param.7) | copy-start | bytes 6291460
  159.3 6.4 %slice-start = ((bf16[4,1245184]{1,0:T(4,128)(2,1)}), bf16[4,196608]{1,0:T(4,128)(2,1)S(1)}, s32[]{:S(2)}) async-start(bf16[4,1245184]{1,0:T(4,128)(2,1)} %reshape.130), calls=%async_computation.12 | async-start | bytes 3145728 | tf_op jit(solution)/shard_map/slice | solution.py:32
  173.9 7.1 %copy-start.2 = (bf16[2048,1024]{1,0:T(8,128)(2,1)S(1)}, bf16[2048,1024]{1,0:T(8,128)(2,1)}, u32[]{:S(2)}) copy-start(bf16[2048,1024]{1,0:T(8,128)(2,1)} %reshape_reshape.3) | copy-start | bytes 12582916
  173.9 7.2 %copy-start.5 = (bf16[1024,1024]{0,1:T(8,128)(2,1)S(1)}, bf16[1024,1024]{0,1:T(8,128)(2,1)}, u32[]{:S(2)}) copy-start(bf16[1024,1024]{0,1:T(8,128)(2,1)} %copy.100) | copy-start | bytes 6291460
  181.1 5.2 copy-start.14
  181.1 5.3 copy-start.6
  186.4 1.9 copy-start.11
  188.3 10.1 %copy-start.9 = (s32[8]{0:T(128)S(1)}, s32[8]{0:T(128)}, u32[]{:S(2)}) copy-start(s32[8]{0:T(128)} %param.12) | copy-start | bytes 100
  190.6 30.4 %all-to-all-start = ((bf16[4,256,768]{2,0,1:T(4,128)(2,1)}), bf16[4,256,768]{2,0,1:T(4,128)(2,1)S(1)}, u32[]{:S(2)}, u32[]{:S(2)}) async-start(bf16[4,256,768]{2,0,1:T(4,128)(2,1)} %copy.77), calls=%async_computation | async-start | bytes 3145728 | tf_op jit(solution)/shard_map/all_to_all | solution.py:82
  198.3 102.2 %reduce-scatter.8.cloned.1.call-start = ((), (), s32[]{:S(2)}) async-start(), calls=%async_computation.10 | async-start | bytes 3932160 | tf_op jit(solution)/shard_map/reduce_scatter | solution.py:62
  224.1 1.2 copy-start.10
  228.4 27.9 %copy-start.12 = (bf16[1024,1024]{0,1:T(8,128)(2,1)S(1)}, bf16[1024,1024]{0,1:T(8,128)(2,1)}, u32[]{:S(2)}) copy-start(bf16[1024,1024]{0,1:T(8,128)(2,1)} %copy-done.11) | copy-start | bytes 6291460
  258.1 2.1 copy-start.7
  260.1 118.1 %reduce-scatter.6.cloned.1.call-start = ((), (), s32[]{:S(2)}) async-start(), calls=%async_computation.9 | async-start | bytes 10485760 | tf_op jit(solution)/shard_map/reduce_scatter | solution.py:62
  262.0 8.3 %copy-start.13 = (bf16[1024,1024]{1,0:T(8,128)(2,1)}, bf16[1024,1024]{1,0:T(8,128)(2,1)S(1)}, u32[]{:S(2)}) copy-start(bf16[1024,1024]{1,0:T(8,128)(2,1)S(1)} %convolution_convert_fusion) | copy-start | bytes 6291460
  274.4 1.6 copy-start.4
  274.4 186.5 %reduce-scatter.4.cloned.1.call-start = ((), (), s32[]{:S(2)}) async-start(), calls=%async_computation.8 | async-start | bytes 10485760 | tf_op jit(solution)/shard_map/reduce_scatter | solution.py:62
  378.3 82.6 %all-to-all-start.3 = ((f32[32,16,1024]{2,1,0:T(8,128)}), f32[32,16,1024]{2,1,0:T(8,128)S(1)}, u32[]{:S(2)}, u32[]{:S(2)}) async-start(f32[32,16,1024]{2,1,0:T(8,128)} %bitcast.116), calls=%async_computation.5 | async-start | bytes 4194304 | tf_op jit(solution)/shard_map/all_to_all | solution.py:18
  460.9 94.4 %copy-start.1 = (f32[8,768]{1,0:T(8,128)S(1)}, f32[8,768]{1,0:T(8,128)}, u32[]{:S(2)}) copy-start(f32[8,768]{1,0:T(8,128)} %param.11) | copy-start | bytes 73732
  460.9 92.0 %all-to-all-start.2 = ((f32[32,8,2048]{2,1,0:T(8,128)}), f32[32,8,2048]{2,1,0:T(8,128)}, u32[]{:S(2)}, u32[]{:S(2)}) async-start(f32[32,8,2048]{2,1,0:T(8,128)} %bitcast.115), calls=%async_computation.3 | async-start | bytes 4194304 | tf_op jit(solution)/shard_map/all_to_all | solution.py:18
Sparse Core Ops, SparseCore 0:
  25.3 99.6 all-gather.2
  260.3 35.2 reduce-scatter.7
  298.0 80.2 reduce-scatter.5
  380.6 80.2 reduce-scatter.3
where the time goes:
time: 573 us; the launch traced here: 563 us
  waiting for transfers between devices  254 us (44%)
  blocking collectives  126 us (22%)
  local copies, waits for them, and re-layouts  76.1 us (13%)
  matrix products  46 us (8%)
  starting transfers between devices  23.4 us (4%)
  other arithmetic  20.4 us (4%)
  between operations  16.8 us (3%)
    reduce_scatter x3, waiting for transfers between devices, weight_sum(): lax.psum_scatter(reordered, 'mp', scatter_dimension=0, tiled=True)  135 us
    all_gather x1, waiting for transfers between devices, one_gather(): lines, at, outs = (lax.all_gather(vector, axis), 0, [])  97.2 us
    psum x1, blocking collectives, per_device(): valid_count = lax.psum(count_part, ('member', 'mp'))  81.5 us
    all_to_all x1, blocking collectives, per_device(): lax.all_to_all(grad_raw, 'member', split_axis=0, concat_axis=1, tiled=True)  26.9 us
    dot_general x3, matrix products, row_outer(): lax.dot_general(left_rows, right_rows, (((0,), (0,)), ((), ())), preferre...  26.8 us
    all_to_all x1, waiting for transfers between devices, per_device(): lax.all_to_all(prediction_lines, 'member', split_axis=1, concat_axis=0, t...  21.9 us
    all_to_all x1, blocking collectives, sent_and_summed(): lax.all_to_all(parts, axis, split_axis=0, concat_axis=0, tiled=True)  17.8 us
    all_to_all x2, starting transfers between devices, sent_and_summed(): lax.all_to_all(parts, axis, split_axis=0, concat_axis=0, tiled=True)  15.4 us
  transfers between devices with their start and end apart: 7, of which 4 were waited for; matrix products, arithmetic and copies ran while one was open for 8% of the time, Pallas kernels for 0%

commit v1 on v0

--- a/solution.py
+++ b/solution.py
@@ -79,8 +79,11 @@
         skip_activation, complete_head, preferred_element_type=jnp.float32
     ).astype(jnp.bfloat16)
     prediction_lines = prediction_lines.reshape(sample_portion, tile_portion, -1)
-    ensemble_reduced = lax.all_to_all(
-        prediction_lines, "member", split_axis=1, concat_axis=0, tiled=True
+    ensemble_reduced = jnp.concatenate(
+        lax.all_to_all(
+            jnp.stack(jnp.split(prediction_lines, lax.axis_size("member"), axis=1)), "member", 0, 0
+        ),
+        axis=0,
     )
     sample_indices = ensemble_reduced.shape[0]
     owned_count = ensemble_reduced.shape[1]

time: 573 us -> 588 us (1.026)
  local copies, waits for them, and re-layouts: 76.1 us -> 94.3 us
    unnamed x35 -> x66, local copies, waits for them, and re-layouts: 12.4 us -> 33.6 us
  transfers between devices with their start and end apart: 7 -> 7, of which waited for: 4 -> 4; matrix products, arithmetic and copies ran while one was open for 8% -> 7% of each run, Pallas kernels for 0% -> 0%
where the time goes in v1:
time: 588 us; the launch traced here: 579 us
  waiting for transfers between devices  252 us (43%)
  blocking collectives  126 us (21%)
  local copies, waits for them, and re-layouts  94.3 us (16%)
  matrix products  46.5 us (8%)
  starting transfers between devices  23.3 us (4%)
  other arithmetic  19.4 us (3%)
  between operations  17 us (3%)
    reduce_scatter x3, waiting for transfers between devices, weight_sum(): lax.psum_scatter(reordered, 'mp', scatter_dimension=0, tiled=True)  135 us
    all_gather x1, waiting for transfers between devices, one_gather(): lines, at, outs = (lax.all_gather(vector, axis), 0, [])  95.7 us
    psum x1, blocking collectives, per_device(): valid_count = lax.psum(count_part, ('member', 'mp'))  81.5 us
    unnamed x66, local copies, waits for them, and re-layouts  33.6 us
    dot_general x3, matrix products, row_outer(): lax.dot_general(left_rows, right_rows, (((0,), (0,)), ((), ())), preferre...  26.8 us
    all_to_all x1, blocking collectives, per_device(): lax.all_to_all(grad_raw, 'member', split_axis=0, concat_axis=1, tiled=True)  26.5 us
    all_to_all x1, waiting for transfers between devices, per_device(): lax.all_to_all(jnp.stack(jnp.split(prediction_lines, lax.axis_size('membe...  21.9 us
    all_to_all x1, blocking collectives, sent_and_summed(): lax.all_to_all(parts, axis, split_axis=0, concat_axis=0, tiled=True)  17.8 us
  transfers between devices with their start and end apart: 7, of which 4 were waited for; matrix products, arithmetic and copies ran while one was open for 7% of the time, Pallas kernels for 0%

profile of v1, /device:TPU:1, one launch (start us, length us, event | category | flops | bytes accessed | tf_op | source)
XLA Modules:
  0.0 578.7 jit_solution(612849403256102766)
XLA Ops:
  9.9 14.1 %pad_maximum_fusion = bf16[1245184]{0:T(1024)(128)(2,1)} fusion(bf16[196608]{0:T(1024)(128)(2,1)S(1)} %reshape.110, bf16[524288]{0:T(1024)(128)(2,1)S(1)} %bitcast.226, bf16[524288]{0:T(1024)(128)(2,1)S(1)} %bitcast.225), kind=kLoop, calls=%fused_computation.31 | loop fusion | flops 7471104 | bytes 4980736 | tf_op jit(solution)/shard_map/concatenate | solution.py:29
  28.1 95.7 %all-gather.3.cloned.1.call-done = bf16[4980736]{0:T(1024)(128)(2,1)} async-done(((bf16[1245184]{0:T(1024)(128)(2,1)}), bf16[4980736]{0:T(1024)(128)(2,1)}) %all-gather.3.cloned.1.call-update) | async-done | bytes 9961488 | tf_op jit(solution)/shard_map/all_gather | solution.py:30
  123.8 13.0 %reshape.134 = bf16[4,1245184]{1,0:T(4,128)(2,1)} reshape(bf16[4980736]{0:T(1024)(128)(2,1)} %all-gather.3.cloned.1.call-done) | data formatting | bytes 19922944 | tf_op jit(solution)/shard_map/all_gather | solution.py:30
  136.8 8.6 %fusion.50 = (bf16[4,524288]{1,0:T(4,128)(2,1)}, bf16[4,524288]{1,0:T(4,128)(2,1)}) fusion(bf16[4,1245184]{1,0:T(4,128)(2,1)} %reshape.134), kind=kLoop, calls=%fused_computation.130 | loop fusion | bytes 16777216 | tf_op jit(solution)/shard_map/slice | solution.py:32
  145.4 8.0 %reshape_reshape.3 = bf16[2048,1024]{1,0:T(8,128)(2,1)} reshape(bf16[4,524288]{1,0:T(4,128)(2,1)} %get-tuple-element.14) | data formatting | bytes 8388608 | tf_op jit(solution)/shard_map/reshape;reshape | solution.py:25
  153.4 5.0 copy.97
  158.4 6.4 %copy.54 = bf16[1024,4,512]{0,2,1:T(8,128)(2,1)} copy(bf16[1024,4,512]{2,0,1:T(8,128)(2,1)} %bitcast.216) | data formatting | bytes 8388608 | tf_op jit(solution)/shard_map/transpose | solution.py:23
  167.6 3.1 reshape.113
  173.1 7.1 %fusion.53 = f32[2048,1024]{1,0:T(8,128)S(1)} fusion(bf16[1024,2048]{0,1:T(8,128)(2,1)} %bitcast.227, bf16[1024,1024]{1,0:T(8,128)(2,1)} %bitcast.228), kind=kOutput, calls=%fused_computation.132 | convolution fusion | flops 4294967296 | bytes 14680064 | tf_op jit(solution)/shard_map/dot_general | solution.py:72
  180.3 5.2 add_convert_fusion
  207.2 7.7 %all-to-all-start = ((bf16[32,4,8,768]{3,2,1,0:T(8,128)(2,1)}), bf16[32,4,8,768]{3,2,1,0:T(8,128)(2,1)S(1)}, u32[]{:S(2)}, u32[]{:S(2)}) async-start(bf16[32,4,8,768]{3,2,1,0:T(8,128)(2,1)} %constant_dynamic-update-slice_fusion), calls=%async_computation | async-start | bytes 3145728 | tf_op jit(solution)/shard_map/all_to_all | solution.py:83
  215.6 21.9 %all-to-all-done = bf16[32,4,8,768]{3,2,1,0:T(8,128)(2,1)S(1)} async-done(((bf16[32,4,8,768]{3,2,1,0:T(8,128)(2,1)}), bf16[32,4,8,768]{3,2,1,0:T(8,128)(2,1)S(1)}, u32[]{:S(2)}, u32[]{:S(2)}) %all-to-all-start) | async-done | bytes 1572896 | tf_op jit(solution)/shard_map/all_to_all | solution.py:83
  240.1 2.8 fusion.20
  243.7 26.5 %all_to_all.35 = bf16[128,8,768]{2,1,0:T(8,128)(2,1)S(1)} all-to-all(bf16[128,8,768]{2,1,0:T(8,128)(2,1)S(1)} %copy.63), channel_id=1, replica_groups=mesh['member'=32,'mp'=4] {'member'}, dimensions={0} | all-to-all | bytes 3145728 | tf_op jit(solution)/shard_map/all_to_all | solution.py:123
  277.7 8.3 %fusion.46 = f32[2048,1024]{1,0:T(8,128)S(1)} fusion(bf16[1024,1024]{1,0:T(8,128)(2,1)S(1)} %convolution_convert_fusion, f32[2048,1024]{1,0:T(8,128)} %copy-done.14), kind=kOutput, calls=%fused_computation.128 | convolution fusion | flops 4313841664 | bytes 18874368 | tf_op jit(solution)/shard_map/dot_general | solution.py:47
  286.0 4.1 copy.68
  291.7 16.7 %fusion.10 = f32[2048,1024]{0,1:T(8,128)} fusion(bf16[1024,1024]{1,0:T(8,128)(2,1)S(1)} %bitcast.230, f32[2048,1024]{1,0:T(8,128)} %copy-done.14, bf16[1024,1024]{1,0:T(8,128)(2,1)} %copy-done.13, bf16[2048,1024]{1,0:T(8,128)(2,1)} %reshape_reshape.3), kind=kOutput, calls=%fused_computation.17 | convolution fusion | flops 8631877632 | bytes 25165824 | tf_op jit(solution)/shard_map/dot_general | solution.py:47
  308.4 7.8 %copy.67 = f32[32,4,8,2048]{3,2,0,1:T(8,128)} copy(f32[32,4,8,2048]{3,2,1,0:T(8,128)} %bitcast.220) | data formatting | bytes 16777216 | tf_op jit(solution)/shard_map/reshape | solution.py:58
  316.2 17.8 %all_to_all.36 = f32[32,8,768]{2,1,0:T(8,128)S(1)} all-to-all(f32[32,8,768]{2,1,0:T(8,128)} %bitcast.271), channel_id=1, replica_groups=mesh['member'=32,'mp'=4] {'member'}, dimensions={0} | all-to-all | bytes 1572864 | tf_op jit(solution)/shard_map/all_to_all | solution.py:18
  334.1 59.7 %reduce-scatter.6.cloned.1.call-done = f32[512,1024]{1,0:T(8,128)} async-done(((f32[2048,1024]{1,0:T(8,128)}), f32[512,1024]{1,0:T(8,128)}) %reduce-scatter.6.cloned.1.call-update) | async-done | bytes 2097168 | tf_op jit(solution)/shard_map/reduce_scatter | solution.py:62
  393.8 7.6 %all-to-all-start.3 = ((f32[32,16,1024]{2,1,0:T(8,128)}), f32[32,16,1024]{2,1,0:T(8,128)S(1)}, u32[]{:S(2)}, u32[]{:S(2)}) async-start(f32[32,16,1024]{2,1,0:T(8,128)} %bitcast.232), calls=%async_computation.5 | async-start | bytes 4194304 | tf_op jit(solution)/shard_map/all_to_all | solution.py:18
  401.4 75.0 %reduce-scatter.4.cloned.1.call-done = f32[256,2048]{1,0:T(8,128)} async-done(((f32[1024,2048]{1,0:T(8,128)}), f32[256,2048]{1,0:T(8,128)}) %reduce-scatter.4.cloned.1.call-update) | async-done | bytes 2097168 | tf_op jit(solution)/shard_map/reduce_scatter | solution.py:62
  476.4 7.7 %all-to-all-start.2 = ((f32[32,8,2048]{2,1,0:T(8,128)}), f32[32,8,2048]{2,1,0:T(8,128)}, u32[]{:S(2)}, u32[]{:S(2)}) async-start(f32[32,8,2048]{2,1,0:T(8,128)} %bitcast.231), calls=%async_computation.3 | async-start | bytes 4194304 | tf_op jit(solution)/shard_map/all_to_all | solution.py:18
  484.1 81.5 %all-reduce = (f32[]{:T(128)}, f32[]{:T(128)}) all-reduce(f32[]{:T(128)} %get-tuple-element.9, f32[]{:T(128)} %get-tuple-element.8), channel_id=1, replica_groups=mesh['member'=32,'mp'=4] {'member','mp'}, use_global_device_ids=true, to_apply=%region_6.7 | all-reduce | flops 2 | bytes 16 | tf_op jit(solution)/shard_map/psum | solution.py:122
  (104 shorter events, 50.6 us)
Async XLA Ops:
  7.2 207.8 %copy-start = (f32[8,768]{1,0:T(8,128)S(1)}, f32[8,768]{1,0:T(8,128)}, u32[]{:S(2)}) copy-start(f32[8,768]{1,0:T(8,128)} %param.11) | copy-start | bytes 73732
  7.2 2.0 copy-start.7
  7.2 2.5 copy-start.8
  7.2 116.6 %all-gather.3.cloned.1.call-start = ((), (), s32[]{:S(2)}) async-start(), calls=%async_computation.11 | async-start | bytes 12451840 | tf_op jit(solution)/shard_map/all_gather | solution.py:30
  24.0 1.6 copy-start.3
  158.4 6.4 %slice-start = ((bf16[4,1245184]{1,0:T(4,128)(2,1)}), bf16[4,196608]{1,0:T(4,128)(2,1)S(1)}, s32[]{:S(2)}) async-start(bf16[4,1245184]{1,0:T(4,128)(2,1)} %reshape.134), calls=%async_computation.12 | async-start | bytes 3145728 | tf_op jit(solution)/shard_map/slice | solution.py:32
  173.1 7.2 %copy-start.2 = (bf16[2048,1024]{1,0:T(8,128)(2,1)S(1)}, bf16[2048,1024]{1,0:T(8,128)(2,1)}, u32[]{:S(2)}) copy-start(bf16[2048,1024]{1,0:T(8,128)(2,1)} %reshape_reshape.3) | copy-start | bytes 12582916
  173.1 7.2 %copy-start.5 = (bf16[1024,1024]{0,1:T(8,128)(2,1)S(1)}, bf16[1024,1024]{0,1:T(8,128)(2,1)}, u32[]{:S(2)}) copy-start(bf16[1024,1024]{0,1:T(8,128)(2,1)} %copy.75) | copy-start | bytes 6291460
  180.2 5.2 copy-start.14
  180.3 5.2 copy-start.6
  185.5 1.9 copy-start.11
  201.0 13.9 %copy-start.9 = (s32[8]{0:T(128)S(1)}, s32[8]{0:T(128)}, u32[]{:S(2)}) copy-start(s32[8]{0:T(128)} %param.12) | copy-start | bytes 100
  207.2 30.3 %all-to-all-start = ((bf16[32,4,8,768]{3,2,1,0:T(8,128)(2,1)}), bf16[32,4,8,768]{3,2,1,0:T(8,128)(2,1)S(1)}, u32[]{:S(2)}, u32[]{:S(2)}) async-start(bf16[32,4,8,768]{3,2,1,0:T(8,128)(2,1)} %constant_dynamic-update-slice_fusion), calls=%async_computation | async-start | bytes 3145728 | tf_op jit(solution)/shard_map/all_to_all | solution.py:83
  214.9 101.4 %reduce-scatter.8.cloned.1.call-start = ((), (), s32[]{:S(2)}) async-start(), calls=%async_computation.10 | async-start | bytes 3932160 | tf_op jit(solution)/shard_map/reduce_scatter | solution.py:62
  238.5 0.9 copy-start.10
  270.2 1.6 copy-start.12
  275.7 118.1 %reduce-scatter.6.cloned.1.call-start = ((), (), s32[]{:S(2)}) async-start(), calls=%async_computation.9 | async-start | bytes 10485760 | tf_op jit(solution)/shard_map/reduce_scatter | solution.py:62
  277.7 8.3 %copy-start.13 = (bf16[1024,1024]{1,0:T(8,128)(2,1)}, bf16[1024,1024]{1,0:T(8,128)(2,1)S(1)}, u32[]{:S(2)}) copy-start(bf16[1024,1024]{1,0:T(8,128)(2,1)S(1)} %convolution_convert_fusion) | copy-start | bytes 6291460
  290.1 1.6 copy-start.4
  290.1 186.3 %reduce-scatter.4.cloned.1.call-start = ((), (), s32[]{:S(2)}) async-start(), calls=%async_computation.8 | async-start | bytes 10485760 | tf_op jit(solution)/shard_map/reduce_scatter | solution.py:62
  393.8 82.6 %all-to-all-start.3 = ((f32[32,16,1024]{2,1,0:T(8,128)}), f32[32,16,1024]{2,1,0:T(8,128)S(1)}, u32[]{:S(2)}, u32[]{:S(2)}) async-start(f32[32,16,1024]{2,1,0:T(8,128)} %bitcast.232), calls=%async_computation.5 | async-start | bytes 4194304 | tf_op jit(solution)/shard_map/all_to_all | solution.py:18
  476.4 91.9 %all-to-all-start.2 = ((f32[32,8,2048]{2,1,0:T(8,128)}), f32[32,8,2048]{2,1,0:T(8,128)}, u32[]{:S(2)}, u32[]{:S(2)}) async-start(f32[32,8,2048]{2,1,0:T(8,128)} %bitcast.231), calls=%async_computation.3 | async-start | bytes 4194304 | tf_op jit(solution)/shard_map/all_to_all | solution.py:18
  567.0 3.7 copy-start.1
Sparse Core Ops, SparseCore 0:
  24.1 99.6 all-gather.2
  275.8 35.2 reduce-scatter.7
  313.6 80.1 reduce-scatter.5
  396.1 80.2 reduce-scatter.3
